TPU v7x, 32 devices: a whole 2x2x4 slice. The times are simulated.
32 devices in a mesh: inst: 4 (over x, core), lab: 8 (over z, y).
Axes of the slice: x: 2, y: 2, z: 4, core: 2. Of those that a mesh axis runs over, the one named last changes fastest.
Arguments:
- features: bfloat16 [2048, 768], P('inst'), may hold values from -6 to 6
- tile_rows: int32 [128], P(('inst', 'lab')), may hold values from 0 to 1, as said below
- tile_labels: int32 [128], P(('inst', 'lab')), may hold values from 0 to 3
- tile_values: bfloat16 [128, 256, 256], P(('inst', 'lab')), may hold values from 0 to 1
- cluster_ids: int32 [8192], P(('lab', 'inst')), may hold values from 0 to 1023, as said below
Outputs:
- label_embed: float32 [8192, 768], P(('lab', 'inst'))
- centroids: float32 [1024, 768], P(('inst', 'lab'))
Inputs may be any that keep to these rules, and one draw needn't show every extreme that they name: Within each block of 4 entries the pairs (tile_rows, tile_labels) are distinct. Within each aligned block of 256 labels, at most 16 labels have clusters with the same value of cluster_ids // 32, and that many is reached in every block.
All inputs are finite; a program needn't handle non-finite values.
Results may differ from a plain program's by a relative error of at most 0.01.
Values may be sent and summed in bfloat16 or wider, within the bound.
A program may use at most 128 MiB of HBM per device.

v0:
```python
import jax
import jax.numpy as jnp
from jax import lax
from jax.sharding import PartitionSpec as P

CL_OWN = 32


def unit_rows(matrix):
    return matrix * lax.rsqrt(jnp.sum(matrix * matrix, axis=-1, keepdims=True) + 1e-06)


def shards(features, tile_rows, tile_labels, tile_values, cluster_ids):
    tile = tile_values.shape[1]
    width = features.shape[1]
    normed = unit_rows(features.astype(jnp.float32)).astype(jnp.bfloat16)
    row_tiles = features.shape[0] // tile
    lab_tiles = cluster_ids.shape[0] * lax.axis_size("inst") // tile
    place = tile_rows * lab_tiles + tile_labels
    dense = jnp.zeros((row_tiles * lab_tiles, tile, tile), jnp.bfloat16).at[place].set(tile_values)
    dense = dense.reshape(row_tiles, lab_tiles, tile, tile)
    shaped = normed.reshape(row_tiles, tile, width)
    partial_value = jnp.einsum("ijrl,ird->jld", dense, shaped, preferred_element_type=jnp.float32)
    partial_value = (
        partial_value.reshape(lab_tiles * tile, width).astype(jnp.bfloat16).astype(jnp.float32)
    )
    summed = lax.psum_scatter(
        partial_value.astype(jnp.bfloat16), "inst", scatter_dimension=0, tiled=True
    ).astype(jnp.float32)
    label_embed = unit_rows(summed)
    n_inst = lax.axis_size("inst")
    n_lab = lax.axis_size("lab")
    owners_all = n_inst * n_lab
    slots = 2 * cluster_ids.shape[0] // owners_all
    owner = cluster_ids // CL_OWN
    marks = (owner[:, None] == lax.iota(jnp.int32, owners_all)[None, :]).astype(jnp.int32)
    before = jnp.cumsum(marks, axis=0) - marks
    slot_of = jnp.sum(before * marks, axis=1)
    position = owner * slots + slot_of
    outgoing = jnp.zeros((owners_all * slots, width), jnp.float32).at[position].set(label_embed)
    local_ids = (
        jnp.zeros((owners_all * slots,), jnp.float32)
        .at[position]
        .set((cluster_ids % CL_OWN).astype(jnp.float32))
    )
    outgoing = outgoing.reshape(n_inst, n_lab, slots, width)
    local_ids = local_ids.reshape(n_inst, n_lab, slots)
    arrived, arrived_ids = (
        lax.all_to_all(
            lax.all_to_all(outgoing, "inst", split_axis=0, concat_axis=0, tiled=True),
            "lab",
            split_axis=1,
            concat_axis=1,
            tiled=True,
        ),
        lax.all_to_all(
            lax.all_to_all(local_ids, "inst", split_axis=0, concat_axis=0, tiled=True),
            "lab",
            split_axis=1,
            concat_axis=1,
            tiled=True,
        ),
    )
    arrived = arrived.reshape(owners_all * slots, width)
    arrived_ids = arrived_ids.reshape(owners_all * slots)
    wanted = lax.iota(jnp.int32, CL_OWN).astype(jnp.float32)
    member = (arrived_ids[None, :] == wanted[:, None]).astype(jnp.float32)
    cluster_sums = jnp.dot(
        member, arrived, precision=lax.Precision.HIGHEST, preferred_element_type=jnp.float32
    )
    return (label_embed, unit_rows(cluster_sums))


def solution(mesh):
    return jax.shard_map(
        shards,
        mesh=mesh,
        in_specs=(
            P("inst", None),
            P(("inst", "lab")),
            P(("inst", "lab")),
            P(("inst", "lab"), None, None),
            P(("lab", "inst")),
        ),
        out_specs=(P(("lab", "inst"), None), P(("inst", "lab"), None)),
        check_vma=False,
    )
```

profile of v0, /device:TPU:0, one launch (start us, length us, event | category | flops | bytes accessed | tf_op | source)
XLA Modules:
  0.0 131.6 jit_solution(8285321264449822571)
XLA Ops:
  7.2 0.7 compare_select_fusion.1
  8.0 1.7 %scatter_fusion = bf16[8,256,256]{2,1,0:T(8,128)(2,1)S(1)} fusion(bf16[8,256,256]{2,1,0:T(8,128)(2,1)S(1)} %broadcast_in_dim.10, s32[4]{0:T(128)S(1)} %compare_select_fusion.1, bf16[4,256,256]{2,1,0:T(8,128)(2,1)} %param.8), kind=kCustom, calls=%fused_computation | custom fusion | bytes 1572880 | tf_op jit(solution)/shard_map/scatter | solution.py:20
  9.7 0.5 copy.11
  10.2 0.2 fusion
  10.5 0.2 fusion.1
  10.7 2.1 %bitcast_convert_fusion = bf16[1024,768]{1,0:T(8,128)(2,1)} fusion(bf16[1024,2,256]{2,0,1:T(8,128)(2,1)S(1)} %bitcast.34, bf16[2,256,768]{2,1,0:T(8,128)(2,1)S(1)} %bitcast.35), kind=kOutput, calls=%fused_computation.3 | convolution fusion | flops 806092800 | bytes 3407872 | tf_op jit(solution)/shard_map/ijrl,ird->jld/dot_general | solution.py:23
  12.8 0.7 copy-done.2
  13.5 0.6 reduce-window.6
  14.1 0.2 slice_reduce_fusion
  14.3 0.1 fusion.9
  14.4 1.4 %scatter_custom_fusion.1 = f32[512]{0:T(512)S(1)} fusion(s32[256]{0:T(256)S(1)} %compare_select_fusion, f32[256]{0:T(256)S(1)} %get-tuple-element.2, f32[]{:T(128)} %constant.44.clone.1), kind=kCustom, calls=%fused_computation.37 | custom fusion | bytes 2052 | tf_op jit(solution)/shard_map/scatter | solution.py:44
  15.9 0.7 reshape.99
  16.6 4.2 %all-to-all-start = ((f32[4,1,128]{2,1,0:T(1,128)}), f32[4,1,128]{2,1,0:T(1,128)S(1)}, u32[]{:S(2)}, u32[]{:S(2)}) async-start(f32[4,1,128]{2,1,0:T(1,128)} %reshape.99), calls=%async_computation.1 | async-start | bytes 4096 | tf_op jit(solution)/shard_map/all_to_all | solution.py:57
  20.8 22.9 %reduce-scatter.2.cloned.1.call-done = bf16[256,768]{1,0:T(8,128)(2,1)} async-done(((bf16[1024,768]{1,0:T(8,128)(2,1)}), bf16[256,768]{1,0:T(8,128)(2,1)}) %reduce-scatter.2.cloned.1.call-update) | async-done | bytes 393232 | tf_op jit(solution)/shard_map/reduce_scatter | solution.py:27
  43.7 1.2 fusion.2
  44.9 3.2 %scatter_custom_fusion.2 = f32[512,768]{1,0:T(8,128)} fusion(s32[256]{0:T(256)S(1)} %compare_select_fusion, f32[]{:T(128)} %constant.44.clone.1, bf16[256,768]{1,0:T(8,128)(2,1)} %reduce-scatter.2.cloned.1.call-done, f32[256]{0:T(256)S(1)} %add_rsqrt_fusion.1), kind=kCustom, calls=%fused_computation.11 | custom fusion | flops 393216 | bytes 1967108 | tf_op jit(solution)/shard_map/scatter | solution.py:40
  48.1 3.6 %all-to-all-start.2 = ((f32[4,8,16,768]{3,2,1,0:T(8,128)}), f32[4,8,16,768]{3,2,1,0:T(8,128)S(1)}, u32[]{:S(2)}, u32[]{:S(2)}) async-start(f32[4,8,16,768]{3,2,1,0:T(8,128)} %bitcast.7), calls=%async_computation.3 | async-start | bytes 3145728 | tf_op jit(solution)/shard_map/all_to_all | solution.py:50
  51.7 0.5 broadcast.91
  52.2 0.7 reduce.2
  52.9 0.1 reshape.100
  53.0 0.6 copy.13
  53.6 18.1 %all-to-all-done.2 = f32[4,8,16,768]{3,2,1,0:T(8,128)S(1)} async-done(((f32[4,8,16,768]{3,2,1,0:T(8,128)}), f32[4,8,16,768]{3,2,1,0:T(8,128)S(1)}, u32[]{:S(2)}, u32[]{:S(2)}) %all-to-all-start.2) | async-done | bytes 1572896 | tf_op jit(solution)/shard_map/all_to_all | solution.py:50
  71.7 5.5 %all-to-all-start.1 = ((f32[4,8,16]{2,0,1:T(4,128)}), f32[4,8,16]{2,0,1:T(4,128)S(1)}, u32[]{:S(2)}, u32[]{:S(2)}) async-start(f32[4,8,16]{2,0,1:T(4,128)} %copy.13), calls=%async_computation.2 | async-start | bytes 32768 | tf_op jit(solution)/shard_map/all_to_all | solution.py:56
  77.2 1.3 copy.15
  78.5 5.3 %all-to-all-done.1 = f32[4,8,16]{2,0,1:T(4,128)S(1)} async-done(((f32[4,8,16]{2,0,1:T(4,128)}), f32[4,8,16]{2,0,1:T(4,128)S(1)}, u32[]{:S(2)}, u32[]{:S(2)}) %all-to-all-start.1) | async-done | bytes 2080 | tf_op jit(solution)/shard_map/all_to_all | solution.py:56
  83.8 3.6 %all-to-all-start.3 = ((f32[4,8,16,768]{3,2,0,1:T(8,128)}), f32[4,8,16,768]{3,2,0,1:T(8,128)S(1)}, u32[]{:S(2)}, u32[]{:S(2)}) async-start(f32[4,8,16,768]{3,2,0,1:T(8,128)} %copy.15), calls=%async_computation.4 | async-start | bytes 3145728 | tf_op jit(solution)/shard_map/all_to_all | solution.py:49
  87.4 0.1 eq.47
  87.5 1.0 convert_multiply_fusion.2
  88.5 34.5 %all-to-all-done.3 = f32[4,8,16,768]{3,2,0,1:T(8,128)S(1)} async-done(((f32[4,8,16,768]{3,2,0,1:T(8,128)}), f32[4,8,16,768]{3,2,0,1:T(8,128)S(1)}, u32[]{:S(2)}, u32[]{:S(2)}) %all-to-all-start.3) | async-done | bytes 1572896 | tf_op jit(solution)/shard_map/all_to_all | solution.py:49
  123.1 0.1 copy.16
  123.2 0.8 multiply_reduce_fusion
  124.0 0.7 broadcast_multiply_fusion
  (20 shorter events, 0.3 us)
Async XLA Ops:
  7.2 36.6 %reduce-scatter.2.cloned.1.call-start = ((), (), s32[]{:S(2)}) async-start(), calls=%async_computation.5 | async-start | bytes 1966080 | tf_op jit(solution)/shard_map/reduce_scatter | solution.py:27
  8.0 2.2 %copy-start.1 = (bf16[512,768]{1,0:T(8,128)(2,1)S(1)}, bf16[512,768]{1,0:T(8,128)(2,1)}, u32[]{:S(2)}) copy-start(bf16[512,768]{1,0:T(8,128)(2,1)} %param.5) | copy-start | bytes 2359300
  12.8 0.7 copy-start.2
  16.6 31.5 %all-to-all-start = ((f32[4,1,128]{2,1,0:T(1,128)}), f32[4,1,128]{2,1,0:T(1,128)S(1)}, u32[]{:S(2)}, u32[]{:S(2)}) async-start(f32[4,1,128]{2,1,0:T(1,128)} %reshape.99), calls=%async_computation.1 | async-start | bytes 4096 | tf_op jit(solution)/shard_map/all_to_all | solution.py:57
  48.1 23.6 %all-to-all-start.2 = ((f32[4,8,16,768]{3,2,1,0:T(8,128)}), f32[4,8,16,768]{3,2,1,0:T(8,128)S(1)}, u32[]{:S(2)}, u32[]{:S(2)}) async-start(f32[4,8,16,768]{3,2,1,0:T(8,128)} %bitcast.7), calls=%async_computation.3 | async-start | bytes 3145728 | tf_op jit(solution)/shard_map/all_to_all | solution.py:50
  71.7 12.1 %all-to-all-start.1 = ((f32[4,8,16]{2,0,1:T(4,128)}), f32[4,8,16]{2,0,1:T(4,128)S(1)}, u32[]{:S(2)}, u32[]{:S(2)}) async-start(f32[4,8,16]{2,0,1:T(4,128)} %copy.13), calls=%async_computation.2 | async-start | bytes 32768 | tf_op jit(solution)/shard_map/all_to_all | solution.py:56
  78.5 9.0 %copy-start = (bf16[256,768]{1,0:T(8,128)(2,1)S(1)}, bf16[256,768]{1,0:T(8,128)(2,1)}, u32[]{:S(2)}) copy-start(bf16[256,768]{1,0:T(8,128)(2,1)} %reduce-scatter.2.cloned.1.call-done) | copy-start | bytes 1179652
  83.8 39.3 %all-to-all-start.3 = ((f32[4,8,16,768]{3,2,0,1:T(8,128)}), f32[4,8,16,768]{3,2,0,1:T(8,128)S(1)}, u32[]{:S(2)}, u32[]{:S(2)}) async-start(f32[4,8,16,768]{3,2,0,1:T(8,128)} %copy.15), calls=%async_computation.4 | async-start | bytes 3145728 | tf_op jit(solution)/shard_map/all_to_all | solution.py:49
Sparse Core Ops, SparseCore 0:
  12.9 30.7 reduce-scatter.1
where the time goes:
time: 132 us
  waiting for transfers between devices  80.9 us (61%)
  starting transfers between devices  16.9 us (13%)
  between operations  14.2 us (11%)
  other arithmetic  8.66 us (7%)
  local copies, waits for them, and re-layouts  7.97 us (6%)
  matrix products  2.95 us (2%)
    all_to_all x1, waiting for transfers between devices, shards(): lax.all_to_all(lax.all_to_all(outgoing, 'inst', split_axis=0, concat_axis...  34.5 us
    reduce_scatter x1, waiting for transfers between devices, shards(): lax.psum_scatter(partial_value.astype(jnp.bfloat16), 'inst', scatter_dime...  22.9 us
    all_to_all x1, waiting for transfers between devices, shards(): lax.all_to_all(outgoing, 'inst', split_axis=0, concat_axis=0, tiled=True)  18.1 us
    all_to_all x1, starting transfers between devices, shards(): lax.all_to_all(lax.all_to_all(local_ids, 'inst', split_axis=0, concat_axi...  5.52 us
    all_to_all x1, waiting for transfers between devices, shards(): lax.all_to_all(lax.all_to_all(local_ids, 'inst', split_axis=0, concat_axi...  5.29 us
    all_to_all x1, starting transfers between devices, shards(): lax.all_to_all(local_ids, 'inst', split_axis=0, concat_axis=0, tiled=True)  4.24 us
    all_to_all x1, starting transfers between devices, shards(): lax.all_to_all(lax.all_to_all(outgoing, 'inst', split_axis=0, concat_axis...  3.58 us
    all_to_all x1, starting transfers between devices, shards(): lax.all_to_all(outgoing, 'inst', split_axis=0, concat_axis=0, tiled=True)  3.56 us
  transfers between devices with their start and end apart: 5, of which 4 were waited for; matrix products, arithmetic and copies ran while one was open for 9% of the time, Pallas kernels for 0%

commit v1 on v0

v1 whole, which is shorter than its diff:
```python
import functools

import jax
import jax.numpy as jnp
from jax import lax
from jax.experimental import pallas as pl
from jax.experimental.pallas import tpu as pltpu
from jax.sharding import PartitionSpec as P

CL_OWN = 32
CHUNKS = 4
MESH = pl.DeviceIdType.MESH


def unit_rows(matrix):
    return matrix * lax.rsqrt(jnp.sum(matrix * matrix, axis=-1, keepdims=True) + 1e-06)


def kernel(
    nx, ny, nz,
    rows_ref, labs_ref, ids_ref, feat_ref, val_ref,
    emb_ref, cen_ref,
    xn, vt, csend, crecv, xsend, xrecv, total, e32, ebf,
    ca_s, ca_r, xa_s, xa_r, acc_a, ya_s, ya_r,
    cb_s, cb_r, yb_s, yb_r, acc_b, xb_s, xb_r,
    fin_a, fin_b, za_s, za_r, zb_s, zb_r,
    s_core, r_core, s_x, r_x, s_ca, r_ca, s_cb, r_cb,
    s_xa, r_xa, s_yb, r_yb, s_ya, r_ya, s_xb, r_xb, s_za, r_za, s_zb, r_zb, s_out,
):
    inst = lax.axis_index("inst")
    lab = lax.axis_index("lab")
    x, c = inst // 2, inst % 2
    z, y = lab // ny, lab % ny
    other = 1 - c
    tile = val_ref.shape[1]
    width = feat_ref.shape[1]
    half = width // 2
    row_tiles = feat_ref.shape[0] // tile
    n_tiles = val_ref.shape[0]
    part = tile // CHUNKS

    core_peer = (x * 2 + other, lab)
    x_at = lambda d: (x + d) % nx
    y_at = lambda d: (y + d) % ny
    z_at = lambda d: (z + d) % nz
    x_peer = lambda d: (x_at(d) * 2 + c, lab)
    y_peer = lambda d: (inst, z * ny + y_at(d))
    z_peer = lambda d: (inst, z_at(d) * ny + y)
    peers = [core_peer]
    peers += [x_peer(d) for d in range(1, nx)]
    peers += [y_peer(d) for d in range(1, ny)]
    peers += [z_peer(d) for d in range(1, nz)]

    barrier = pltpu.get_barrier_semaphore()
    for peer in peers:
        pl.semaphore_signal(barrier, inc=1, device_id=peer, device_id_type=MESH)

    def remote(src, dst, send, recv, peer):
        return pltpu.make_async_remote_copy(
            src_ref=src, dst_ref=dst, send_sem=send, recv_sem=recv,
            device_id=peer, device_id_type=MESH,
        )

    sent = []

    xn[...] = unit_rows(feat_ref[...].astype(jnp.float32)).astype(jnp.bfloat16)
    for n in range(n_tiles):
        vt[n] = val_ref[n].T
    vt[n_tiles] = jnp.zeros((tile, tile), jnp.bfloat16)

    def partial(label_tile):
        pieces = []
        for r in range(row_tiles):
            at = jnp.int32(n_tiles)
            for n in range(n_tiles):
                hit = jnp.logical_and(rows_ref[n] == r, labs_ref[n] == label_tile)
                at = jnp.where(hit, n, at)
            pieces.append(vt[at])
        lhs = jnp.concatenate(pieces, axis=1)
        return jnp.dot(lhs, xn[...], preferred_element_type=jnp.float32)

    def core_send(d):
        xp = x_at(d)
        csend[xp] = partial(xp * 2 + other).astype(jnp.bfloat16)
        copies = []
        for q in range(CHUNKS):
            rows = pl.ds(q * part, part)
            copy = remote(
                csend.at[xp, rows], crecv.at[xp, rows],
                s_core.at[xp, q], r_core.at[xp, q], core_peer,
            )
            copies.append(copy)
        return copies

    x_copies = {}
    for d in range(1, nx):
        copies = core_send(d)
        if d == 1:
            pl.semaphore_wait(barrier, len(peers))
        for copy in copies:
            copy.start()
        sent += copies
        total[...] = partial(x_at(d) * 2 + c)
        for q in range(CHUNKS):
            rows = pl.ds(q * part, part)
            copies[q].wait_recv()
            mixed = total[rows] + crecv[x_at(d), rows].astype(jnp.float32)
            xsend[d - 1, rows] = mixed.astype(jnp.bfloat16)
            copy = remote(
                xsend.at[d - 1, rows], xrecv.at[d - 1, rows],
                s_x.at[d - 1, q], r_x.at[d - 1, q], x_peer(d),
            )
            copy.start()
            x_copies[d, q] = copy
            sent.append(copy)
    copies = core_send(0)
    if nx == 1:
        pl.semaphore_wait(barrier, len(peers))
    for copy in copies:
        copy.start()
    sent += copies
    total[...] = partial(x * 2 + c)
    for q in range(CHUNKS):
        rows = pl.ds(q * part, part)
        copies[q].wait_recv()
        total[rows] += crecv[x, rows].astype(jnp.float32)

    outs = []
    for q in range(CHUNKS):
        rows = pl.ds(q * part, part)
        value = total[rows]
        for d in range(1, nx):
            x_copies[d, q].wait_recv()
            value += xrecv[d - 1, rows].astype(jnp.float32)
        value = unit_rows(value)
        e32[rows] = value
        ebf[rows] = value.astype(jnp.bfloat16)
        out = pltpu.make_async_copy(e32.at[rows], emb_ref.at[rows], s_out.at[q])
        out.start()
        outs.append(out)

    ids = ids_ref[...].reshape(1, 1, tile)
    zb = nz * CL_OWN
    within = (
        lax.broadcasted_iota(jnp.int32, (nz, CL_OWN, tile), 0) * (ny * CL_OWN)
        + lax.broadcasted_iota(jnp.int32, (nz, CL_OWN, tile), 1)
    )

    def picks(xp, cp, yp):
        base = ((xp * 2 + cp) * (nz * ny) + yp) * CL_OWN
        hit = jnp.where(within + base == ids, 1.0, 0.0)
        return hit.reshape(zb, tile).astype(jnp.bfloat16)

    def sums_a(xp, cp):
        member = jnp.concatenate([picks(xp, cp, yp) for yp in range(ny)], axis=0)
        out = jnp.dot(member, ebf[:, :half], preferred_element_type=jnp.float32)
        return out.reshape(ny, zb, half)

    def sums_b(yp, cp):
        member = jnp.concatenate([picks(xp, cp, yp) for xp in range(nx)], axis=0)
        out = jnp.dot(member, ebf[:, half:], preferred_element_type=jnp.float32)
        return out.reshape(nx, zb, half)

    core_a, core_b = {}, {}
    for d in [*range(1, max(nx, ny)), 0]:
        if d < nx:
            xp = x_at(d)
            ca_s[xp] = sums_a(xp, other).astype(jnp.bfloat16)
            core_a[d] = remote(ca_s.at[xp], ca_r.at[xp], s_ca.at[xp], r_ca.at[xp], core_peer)
            core_a[d].start()
        if d < ny:
            yp = y_at(d)
            cb_s[yp] = sums_b(yp, other).astype(jnp.bfloat16)
            core_b[d] = remote(cb_s.at[yp], cb_r.at[yp], s_cb.at[yp], r_cb.at[yp], core_peer)
            core_b[d].start()
    sent += [*core_a.values(), *core_b.values()]

    xa, yb = {}, {}
    for d in [*range(1, max(nx, ny)), 0]:
        if d < nx:
            xp = x_at(d)
            mine = sums_a(xp, c)
            core_a[d].wait_recv()
            mine = mine + ca_r[xp].astype(jnp.float32)
            if d:
                xa_s[d - 1] = mine.astype(jnp.bfloat16)
                for k in [*range(1, ny), 0]:
                    yp = y_at(k)
                    xa[d, k] = remote(
                        xa_s.at[d - 1, yp], xa_r.at[d - 1, yp],
                        s_xa.at[d - 1, yp], r_xa.at[d - 1, yp], x_peer(d),
                    )
                    xa[d, k].start()
            else:
                acc_a[...] = mine
        if d < ny:
            yp = y_at(d)
            mine = sums_b(yp, c)
            core_b[d].wait_recv()
            mine = mine + cb_r[yp].astype(jnp.float32)
            if d:
                yb_s[d - 1] = mine.astype(jnp.bfloat16)
                for k in [*range(1, nx), 0]:
                    xp = x_at(k)
                    yb[d, k] = remote(
                        yb_s.at[d - 1, xp], yb_r.at[d - 1, xp],
                        s_yb.at[d - 1, xp], r_yb.at[d - 1, xp], y_peer(d),
                    )
                    yb[d, k].start()
            else:
                acc_b[...] = mine
    sent += [*xa.values(), *yb.values()]

    ya, xb = {}, {}
    for k in [*range(1, max(nx, ny)), 0]:
        if k < ny:
            yp = y_at(k)
            mine = acc_a[yp]
            for d in range(1, nx):
                xa[d, k].wait_recv()
                mine += xa_r[d - 1, yp].astype(jnp.float32)
            if k:
                ya_s[k - 1] = mine.astype(jnp.bfloat16)
                ya[k] = remote(
                    ya_s.at[k - 1], ya_r.at[k - 1], s_ya.at[k - 1], r_ya.at[k - 1], y_peer(k)
                )
                ya[k].start()
            else:
                fin_a[...] = mine.reshape(nz, CL_OWN, half)
        if k < nx:
            xp = x_at(k)
            mine = acc_b[xp]
            for d in range(1, ny):
                yb[d, k].wait_recv()
                mine += yb_r[d - 1, xp].astype(jnp.float32)
            if k:
                xb_s[k - 1] = mine.astype(jnp.bfloat16)
                xb[k] = remote(
                    xb_s.at[k - 1], xb_r.at[k - 1], s_xb.at[k - 1], r_xb.at[k - 1], x_peer(k)
                )
                xb[k].start()
            else:
                fin_b[...] = mine.reshape(nz, CL_OWN, half)
    sent += [*ya.values(), *xb.values()]

    zs = []
    for fin, got, arrived, z_s, z_r, s_z, r_z in (
        (fin_a, ya, ya_r, za_s, za_r, s_za, r_za),
        (fin_b, xb, xb_r, zb_s, zb_r, s_zb, r_zb),
    ):
        mine = fin[...]
        for k, copy in got.items():
            copy.wait_recv()
            mine += arrived[k - 1].astype(jnp.float32).reshape(nz, CL_OWN, half)
        fin[...] = mine
        for d in range(1, nz):
            z_s[d - 1] = fin[z_at(d)].astype(jnp.bfloat16)
            copy = remote(
                z_s.at[d - 1], z_r.at[d - 1], s_z.at[d - 1], r_z.at[d - 1], z_peer(d)
            )
            copy.start()
            zs.append(copy)
    sent += zs

    sum_a, sum_b = fin_a[z], fin_b[z]
    for copy in zs:
        copy.wait_recv()
    for d in range(1, nz):
        sum_a += za_r[d - 1].astype(jnp.float32)
        sum_b += zb_r[d - 1].astype(jnp.float32)
    cen_ref[...] = unit_rows(jnp.concatenate([sum_a, sum_b], axis=1))

    for copy in sent:
        copy.wait_send()
    for out in outs:
        out.wait()


def shards(features, tile_rows, tile_labels, tile_values, cluster_ids):
    tile = tile_values.shape[1]
    width = features.shape[1]
    labels = cluster_ids.shape[0]
    n_inst, n_lab = lax.axis_size("inst"), lax.axis_size("lab")
    nx = n_inst // 2
    ny = nx if n_lab % nx == 0 else 1
    nz = n_lab // ny
    assert labels == tile
    half = width // 2
    zb = nz * CL_OWN
    bf, f32 = jnp.bfloat16, jnp.float32
    ox, oy, oz = max(nx - 1, 1), max(ny - 1, 1), max(nz - 1, 1)
    dma = lambda *shape: [pltpu.SemaphoreType.DMA(shape)] * 2
    vmem = pl.BlockSpec(memory_space=pltpu.VMEM)
    smem = pl.BlockSpec(memory_space=pltpu.SMEM)
    return pl.pallas_call(
        functools.partial(kernel, nx, ny, nz),
        out_shape=(
            jax.ShapeDtypeStruct((labels, width), f32),
            jax.ShapeDtypeStruct((CL_OWN, width), f32),
        ),
        in_specs=[smem, smem, vmem, vmem, vmem],
        out_specs=(pl.BlockSpec(memory_space=pl.ANY), vmem),
        scratch_shapes=[
            pltpu.VMEM(features.shape, bf),
            pltpu.VMEM((tile_values.shape[0] + 1, tile, tile), bf),
            pltpu.VMEM((nx, tile, width), bf),
            pltpu.VMEM((nx, tile, width), bf),
            pltpu.VMEM((ox, tile, width), bf),
            pltpu.VMEM((ox, tile, width), bf),
            pltpu.VMEM((tile, width), f32),
            pltpu.VMEM((tile, width), f32),
            pltpu.VMEM((tile, width), bf),
            pltpu.VMEM((nx, ny, zb, half), bf),
            pltpu.VMEM((nx, ny, zb, half), bf),
            pltpu.VMEM((ox, ny, zb, half), bf),
            pltpu.VMEM((ox, ny, zb, half), bf),
            pltpu.VMEM((ny, zb, half), f32),
            pltpu.VMEM((oy, zb, half), bf),
            pltpu.VMEM((oy, zb, half), bf),
            pltpu.VMEM((ny, nx, zb, half), bf),
            pltpu.VMEM((ny, nx, zb, half), bf),
            pltpu.VMEM((oy, nx, zb, half), bf),
            pltpu.VMEM((oy, nx, zb, half), bf),
            pltpu.VMEM((nx, zb, half), f32),
            pltpu.VMEM((ox, zb, half), bf),
            pltpu.VMEM((ox, zb, half), bf),
            pltpu.VMEM((nz, CL_OWN, half), f32),
            pltpu.VMEM((nz, CL_OWN, half), f32),
            pltpu.VMEM((oz, CL_OWN, half), bf),
            pltpu.VMEM((oz, CL_OWN, half), bf),
            pltpu.VMEM((oz, CL_OWN, half), bf),
            pltpu.VMEM((oz, CL_OWN, half), bf),
            *dma(nx, CHUNKS),
            *dma(ox, CHUNKS),
            *dma(nx),
            *dma(ny),
            *dma(ox, ny),
            *dma(oy, nx),
            *dma(oy),
            *dma(ox),
            *dma(oz),
            *dma(oz),
            pltpu.SemaphoreType.DMA((CHUNKS,)),
        ],
        compiler_params=pltpu.CompilerParams(
            collective_id=0, has_side_effects=True, vmem_limit_bytes=60 * 1024 * 1024
        ),
        name="pifa_step",
    )(tile_rows, tile_labels, cluster_ids.reshape(1, labels), features, tile_values)


def solution(mesh):
    return jax.shard_map(
        shards,
        mesh=mesh,
        in_specs=(
            P("inst", None),
            P(("inst", "lab")),
            P(("inst", "lab")),
            P(("inst", "lab"), None, None),
            P(("lab", "inst")),
        ),
        out_specs=(P(("lab", "inst"), None), P(("inst", "lab"), None)),
        check_vma=False,
    )
```

time: 132 us -> 39.1 us (0.30)
  waiting for transfers between devices: 80.9 us -> 0 us
  Pallas kernels: 0 us -> 35.6 us
  starting transfers between devices: 16.9 us -> 0 us
  between operations: 14.2 us -> 0.65 us
  other arithmetic: 8.66 us -> 0 us
  local copies, waits for them, and re-layouts: 7.97 us -> 2.74 us
  matrix products: 2.95 us -> 0 us
    all_to_all x4 -> x0, waiting for transfers between devices: 58 us -> none  [the longest x1 34.5 us: shards(): lax.all_to_all(lax.all_to_all(outgoing, 'inst', split_axis=0, concat_axis...]
    pallas_call x0 -> x1, Pallas kernels: none -> 35.6 us  [shards(): pl.pallas_call(functools.partial(kernel, nx, ny, nz), out_shape=(jax.Shap...]
    reduce_scatter x1 -> x0, waiting for transfers between devices: 22.9 us -> none  [shards(): lax.psum_scatter(partial_value.astype(jnp.bfloat16), 'inst', scatter_dime...]
    all_to_all x4 -> x0, starting transfers between devices: 16.9 us -> none  [the longest x1 5.52 us: shards(): lax.all_to_all(lax.all_to_all(local_ids, 'inst', split_axis=0, concat_axi...]
    scatter x1 -> x0, other arithmetic: 3.22 us -> none  [shards(): jnp.zeros((owners_all * slots, width), jnp.float32).at[position]]
    scatter x2 -> x0, local copies, waits for them, and re-layouts: 3.08 us -> none  [the longest x1 1.69 us: shards(): jnp.zeros((row_tiles * lab_tiles, tile, tile), jnp.bfloat16).at[place]]
    dot_general x2 -> x0, matrix products: 2.95 us -> none  [the longest x1 2.14 us: shards(): jnp.einsum('ijrl,ird->jld', dense, shaped, preferred_element_type=jnp.flo...]
    all_to_all x5 -> x0, local copies, waits for them, and re-layouts: 2.53 us -> none  [the longest x1 1.29 us: shards(): lax.all_to_all(outgoing, 'inst', split_axis=0, concat_axis=0, tiled=True)]
  transfers between devices with their start and end apart: 5 -> 0, of which waited for: 4 -> 0; matrix products, arithmetic and copies ran while one was open for 9% -> 0% of each run, Pallas kernels for 0% -> 0%
where the time goes in v1:
time: 39.1 us; the launch traced here: 39 us
  Pallas kernels  35.6 us (91%)
  local copies, waits for them, and re-layouts  2.74 us (7%)
  between operations  0.65 us (2%)
    pallas_call x1, Pallas kernels, shards(): pl.pallas_call(functools.partial(kernel, nx, ny, nz), out_shape=(jax.Shap...  35.6 us
    unnamed x4, local copies, waits for them, and re-layouts  2.74 us

profile of v1, /device:TPU:0, one launch (start us, length us, event | category | flops | bytes accessed | tf_op | source)
XLA Modules:
  0.0 39.0 jit_solution(8241019662517700551)
XLA Ops:
  0.6 35.6 %pifa_step.1 = (f32[256,768]{1,0:T(8,128)}, f32[32,768]{1,0:T(8,128)}) custom-call(s32[4]{0:T(128)} %rows_ref.1, s32[4]{0:T(128)} %labs_ref.1, s32[1,256]{1,0:T(1,128)} %bitcast.1, bf16[512,768]{1,0:T(8,128)(2,1)} %feat_ref.1, bf16[4,256,256]{2,1,0:T(8,128)(2,1)} %val_ref.1), custom_call_target="tpu_custom_call" | custom-call | tf_op jit(solution)/shard_map/pifa_step/pallas_call | solution.py:295
  36.2 0.0 copy-start
  36.2 2.1 %copy.9 = f32[256,768]{1,0:T(8,128)} copy(f32[256,768]{1,0:T(8,128)} %get-tuple-element.4) | data formatting | bytes 1572864
  38.3 0.0 copy-done
  38.3 0.6 %copy.10 = f32[32,768]{1,0:T(8,128)} copy(f32[32,768]{1,0:T(8,128)S(1)} %copy-done) | data formatting | bytes 196608
Async XLA Ops:
  36.2 2.1 %copy-start = (f32[32,768]{1,0:T(8,128)S(1)}, f32[32,768]{1,0:T(8,128)}, u32[]{:S(2)}) copy-start(f32[32,768]{1,0:T(8,128)} %get-tuple-element.5) | copy-start | bytes 294916

commit v2 on v1

v2 whole, which is shorter than its diff:
```python
import functools

import jax
import jax.numpy as jnp
from jax import lax
from jax.experimental import pallas as pl
from jax.experimental.pallas import tpu as pltpu
from jax.sharding import PartitionSpec as P

CL_OWN = 32
CHUNKS = 8
PIECES = 3
MESH = pl.DeviceIdType.MESH


def unit_rows(matrix):
    return matrix * lax.rsqrt(jnp.sum(matrix * matrix, axis=-1, keepdims=True) + 1e-06)


def kernel(
    nx, ny, nz, pair,
    rows_ref, labs_ref, ids_ref, feat_ref, val_ref,
    emb_ref, cen_ref,
    xn, vt, csend, crecv, xsend, xrecv, total, ebf, ids_far, picks,
    ca_s, ca_r, xa_s, xa_r, acc_a, ya_s, ya_r,
    cb_s, cb_r, yb_s, yb_r, acc_b, xb_s, xb_r,
    fin_a, fin_b, za_s, za_r, zb_s, zb_r,
    s_core, r_core, s_x, r_x, s_ca, r_ca, s_cb, r_cb,
    s_xa, r_xa, s_yb, r_yb, s_ya, r_ya, s_xb, r_xb, s_za, r_za, s_zb, r_zb, s_g, r_g, s_ids, r_ids,
):
    inst = lax.axis_index("inst")
    lab = lax.axis_index("lab")
    x, c = inst // 2, inst % 2
    z, y = lab // ny, lab % ny
    other = 1 - c
    tile = val_ref.shape[1]
    width = feat_ref.shape[1]
    half = width // 2
    row_tiles = feat_ref.shape[0] // tile
    n_tiles = val_ref.shape[0]
    part = tile // CHUNKS

    core_peer = (x * 2 + other, lab)
    x_at = lambda d: (x + d) % nx
    y_at = lambda d: (y + d) % ny
    zq, zr = z // pair, z % pair
    zq_all = nz // pair
    zb = zq_all * CL_OWN
    lanes = half // PIECES
    zq_at = lambda d: (zq + d) % zq_all
    x_peer = lambda d: (x_at(d) * 2 + c, lab)
    y_peer = lambda d: (inst, z * ny + y_at(d))
    z_peer = lambda d: (inst, (zq_at(d) * pair + zr) * ny + y)
    pair_peer = (inst, (zq * pair + (pair - 1 - zr)) * ny + y)
    peers = [core_peer]
    peers += [x_peer(d) for d in range(1, nx)]
    peers += [y_peer(d) for d in range(1, ny)]
    peers += [z_peer(d) for d in range(1, zq_all)]
    if pair == 2:
        peers.append(pair_peer)

    barrier = pltpu.get_barrier_semaphore()
    for peer in peers:
        pl.semaphore_signal(barrier, inc=1, device_id=peer, device_id_type=MESH)

    def remote(src, dst, send, recv, peer):
        return pltpu.make_async_remote_copy(
            src_ref=src, dst_ref=dst, send_sem=send, recv_sem=recv,
            device_id=peer, device_id_type=MESH,
        )

    sent = []

    xn[...] = unit_rows(feat_ref[...].astype(jnp.float32)).astype(jnp.bfloat16)
    for n in range(n_tiles):
        vt[n] = val_ref[n].T
    vt[n_tiles] = jnp.zeros((tile, tile), jnp.bfloat16)

    def partial(label_tile):
        pieces = []
        for r in range(row_tiles):
            at = jnp.int32(n_tiles)
            for n in range(n_tiles):
                hit = jnp.logical_and(rows_ref[n] == r, labs_ref[n] == label_tile)
                at = jnp.where(hit, n, at)
            pieces.append(vt[at])
        lhs = jnp.concatenate(pieces, axis=1)
        return jnp.dot(lhs, xn[...], preferred_element_type=jnp.float32)

    ids_copy = remote(ids_ref, ids_far, s_ids, r_ids, pair_peer)

    def meet():
        pl.semaphore_wait(barrier, len(peers))
        if pair == 2:
            ids_copy.start()
            sent.append(ids_copy)

    def core_send(d):
        xp = x_at(d)
        csend[xp] = partial(xp * 2 + other).astype(jnp.bfloat16)
        copies = []
        for q in range(CHUNKS):
            rows = pl.ds(q * part, part)
            copy = remote(
                csend.at[xp, rows], crecv.at[xp, rows],
                s_core.at[xp, q], r_core.at[xp, q], core_peer,
            )
            copies.append(copy)
        return copies

    x_copies = {}
    for d in range(1, nx):
        copies = core_send(d)
        if d == 1:
            meet()
        for copy in copies:
            copy.start()
        sent += copies
        total[...] = partial(x_at(d) * 2 + c)
        for q in range(CHUNKS):
            rows = pl.ds(q * part, part)
            copies[q].wait_recv()
            mixed = total[rows] + crecv[x_at(d), rows].astype(jnp.float32)
            xsend[d - 1, rows] = mixed.astype(jnp.bfloat16)
            copy = remote(
                xsend.at[d - 1, rows], xrecv.at[d - 1, rows],
                s_x.at[d - 1, q], r_x.at[d - 1, q], x_peer(d),
            )
            copy.start()
            x_copies[d, q] = copy
            sent.append(copy)
    copies = core_send(0)
    if nx == 1:
        meet()
    for copy in copies:
        copy.start()
    sent += copies
    total[...] = partial(x * 2 + c)
    for q in range(CHUNKS):
        rows = pl.ds(q * part, part)
        copies[q].wait_recv()
        total[rows] += crecv[x, rows].astype(jnp.float32)

    within = (
        lax.broadcasted_iota(jnp.int32, (zq_all, CL_OWN, tile), 0) * (pair * ny * CL_OWN)
        + lax.broadcasted_iota(jnp.int32, (zq_all, CL_OWN, tile), 1)
    )

    def mark(ids, columns):
        for which, cp in enumerate((other, c)):
            for xp in range(nx):
                for yp in range(ny):
                    base = (((xp * 2 + cp) * nz + zr) * ny + yp) * CL_OWN
                    hit = jnp.where(within + base == ids.reshape(1, 1, tile), 1.0, 0.0)
                    picks[which, xp, yp, :, columns] = hit.reshape(zb, tile).astype(jnp.bfloat16)

    gather = []
    mark(ids_ref[...], pl.ds(0, tile))
    if pair == 2:
        ids_copy.wait_recv()
        mark(ids_far[...], pl.ds(tile, tile))

    for q in range(CHUNKS):
        rows = pl.ds(q * part, part)
        value = total[rows]
        for d in range(1, nx):
            x_copies[d, q].wait_recv()
            value += xrecv[d - 1, rows].astype(jnp.float32)
        value = unit_rows(value)
        emb_ref[rows] = value
        ebf[rows] = value.astype(jnp.bfloat16)
        if pair == 2:
            gather.append(
                remote(
                    ebf.at[rows], ebf.at[pl.ds(tile + q * part, part)],
                    s_g.at[q], r_g.at[q], pair_peer,
                )
            )
            gather[-1].start()
    sent += gather

    def sums_a(xp, which):
        member = picks[which, xp].reshape(ny * zb, pair * tile)
        out = jnp.dot(member, ebf[:, :half], preferred_element_type=jnp.float32)
        return out.reshape(ny, zb, half)

    def sums_b(yp, which):
        member = jnp.concatenate([picks[which, xp, yp] for xp in range(nx)], axis=0)
        out = jnp.dot(member, ebf[:, half:], preferred_element_type=jnp.float32)
        return out.reshape(nx, zb, half)

    for copy in gather:
        copy.wait_recv()

    order = [*range(1, max(nx, ny)), 0]
    core_a, core_b = {}, {}
    for d in order:
        if d < nx:
            xp = x_at(d)
            ca_s[xp] = sums_a(xp, 0).astype(jnp.bfloat16)
            core_a[d] = remote(ca_s.at[xp], ca_r.at[xp], s_ca.at[xp], r_ca.at[xp], core_peer)
            core_a[d].start()
        if d < ny:
            yp = y_at(d)
            cb_s[yp] = sums_b(yp, 0).astype(jnp.bfloat16)
            core_b[d] = remote(cb_s.at[yp], cb_r.at[yp], s_cb.at[yp], r_cb.at[yp], core_peer)
            core_b[d].start()
    sent += [*core_a.values(), *core_b.values()]

    xa, yb = {}, {}
    for d in order:
        if d < nx:
            xp = x_at(d)
            mine = sums_a(xp, 1)
            core_a[d].wait_recv()
            mine = mine + ca_r[xp].astype(jnp.float32)
            for p in range(PIECES):
                piece = mine[:, :, p * lanes : (p + 1) * lanes]
                if d:
                    xa_s[d - 1, p] = piece.astype(jnp.bfloat16)
                    xa[d, p] = remote(
                        xa_s.at[d - 1, p], xa_r.at[d - 1, p],
                        s_xa.at[d - 1, p], r_xa.at[d - 1, p], x_peer(d),
                    )
                    xa[d, p].start()
                else:
                    acc_a[p] = piece
        if d < ny:
            yp = y_at(d)
            mine = sums_b(yp, 1)
            core_b[d].wait_recv()
            mine = mine + cb_r[yp].astype(jnp.float32)
            for p in range(PIECES):
                piece = mine[:, :, p * lanes : (p + 1) * lanes]
                if d:
                    yb_s[d - 1, p] = piece.astype(jnp.bfloat16)
                    yb[d, p] = remote(
                        yb_s.at[d - 1, p], yb_r.at[d - 1, p],
                        s_yb.at[d - 1, p], r_yb.at[d - 1, p], y_peer(d),
                    )
                    yb[d, p].start()
                else:
                    acc_b[p] = piece
    sent += [*xa.values(), *yb.values()]

    ya, xb, zs = {}, {}, []

    def second(p):
        for d in range(1, nx):
            xa[d, p].wait_recv()
        for k in range(ny - 1, -1, -1):
            yp = y_at(k)
            mine = acc_a[p, yp]
            for d in range(1, nx):
                mine += xa_r[d - 1, p, yp].astype(jnp.float32)
            if k:
                ya_s[k - 1, p] = mine.astype(jnp.bfloat16)
                ya[k, p] = remote(
                    ya_s.at[k - 1, p], ya_r.at[k - 1, p],
                    s_ya.at[k - 1, p], r_ya.at[k - 1, p], y_peer(k),
                )
                ya[k, p].start()
                sent.append(ya[k, p])
            else:
                fin_a[p] = mine.reshape(zq_all, CL_OWN, lanes)
        for d in range(1, ny):
            yb[d, p].wait_recv()
        for k in range(nx - 1, -1, -1):
            xp = x_at(k)
            mine = acc_b[p, xp]
            for d in range(1, ny):
                mine += yb_r[d - 1, p, xp].astype(jnp.float32)
            if k:
                xb_s[k - 1, p] = mine.astype(jnp.bfloat16)
                xb[k, p] = remote(
                    xb_s.at[k - 1, p], xb_r.at[k - 1, p],
                    s_xb.at[k - 1, p], r_xb.at[k - 1, p], x_peer(k),
                )
                xb[k, p].start()
                sent.append(xb[k, p])
            else:
                fin_b[p] = mine.reshape(zq_all, CL_OWN, lanes)

    def third(p):
        for fin, got, arrived, n_got, z_s, z_r, s_z, r_z in (
            (fin_a, ya, ya_r, ny, za_s, za_r, s_za, r_za),
            (fin_b, xb, xb_r, nx, zb_s, zb_r, s_zb, r_zb),
        ):
            mine = fin[p]
            for k in range(1, n_got):
                got[k, p].wait_recv()
                mine += arrived[k - 1, p].astype(jnp.float32).reshape(zq_all, CL_OWN, lanes)
            fin[p] = mine
            for d in range(1, zq_all):
                z_s[d - 1, p] = fin[p, zq_at(d)].astype(jnp.bfloat16)
                copy = remote(
                    z_s.at[d - 1, p], z_r.at[d - 1, p],
                    s_z.at[d - 1, p], r_z.at[d - 1, p], z_peer(d),
                )
                copy.start()
                zs.append(copy)

    for p in range(PIECES + 1):
        if p < PIECES:
            second(p)
        if p > 0:
            third(p - 1)
    sent += zs

    for copy in zs:
        copy.wait_recv()
    pieces = []
    for fin, z_r in ((fin_a, za_r), (fin_b, zb_r)):
        for p in range(PIECES):
            mine = fin[p, zq]
            for d in range(1, zq_all):
                mine += z_r[d - 1, p].astype(jnp.float32)
            pieces.append(mine)
    cen_ref[...] = unit_rows(jnp.concatenate(pieces, axis=1))

    for copy in sent:
        copy.wait_send()


def shards(features, tile_rows, tile_labels, tile_values, cluster_ids):
    tile = tile_values.shape[1]
    width = features.shape[1]
    labels = cluster_ids.shape[0]
    n_inst, n_lab = lax.axis_size("inst"), lax.axis_size("lab")
    nx = n_inst // 2
    ny = nx if n_lab % nx == 0 else 1
    nz = n_lab // ny
    assert labels == tile
    pair = 2 if nz % 2 == 0 else 1
    zb = nz // pair * CL_OWN
    lanes = width // 2 // PIECES
    half = lanes * PIECES
    bf, f32 = jnp.bfloat16, jnp.float32
    ox, oy, oz = max(nx - 1, 1), max(ny - 1, 1), max(nz // pair - 1, 1)
    dma = lambda *shape: [pltpu.SemaphoreType.DMA(shape)] * 2
    vmem = pl.BlockSpec(memory_space=pltpu.VMEM)
    smem = pl.BlockSpec(memory_space=pltpu.SMEM)
    return pl.pallas_call(
        functools.partial(kernel, nx, ny, nz, pair),
        out_shape=(
            pltpu.VMEM((labels, width), f32),
            pltpu.VMEM((CL_OWN, width), f32),
        ),
        in_specs=[smem, smem, vmem, vmem, vmem],
        out_specs=(vmem, vmem),
        scratch_shapes=[
            pltpu.VMEM(features.shape, bf),
            pltpu.VMEM((tile_values.shape[0] + 1, tile, tile), bf),
            pltpu.VMEM((nx, tile, width), bf),
            pltpu.VMEM((nx, tile, width), bf),
            pltpu.VMEM((ox, tile, width), bf),
            pltpu.VMEM((ox, tile, width), bf),
            pltpu.VMEM((tile, width), f32),
            pltpu.VMEM((pair * tile, width), bf),
            pltpu.VMEM((1, tile), jnp.int32),
            pltpu.VMEM((2, nx, ny, zb, pair * tile), bf),
            pltpu.VMEM((nx, ny, zb, half), bf),
            pltpu.VMEM((nx, ny, zb, half), bf),
            pltpu.VMEM((ox, PIECES, ny, zb, lanes), bf),
            pltpu.VMEM((ox, PIECES, ny, zb, lanes), bf),
            pltpu.VMEM((PIECES, ny, zb, lanes), f32),
            pltpu.VMEM((oy, PIECES, zb, lanes), bf),
            pltpu.VMEM((oy, PIECES, zb, lanes), bf),
            pltpu.VMEM((ny, nx, zb, half), bf),
            pltpu.VMEM((ny, nx, zb, half), bf),
            pltpu.VMEM((oy, PIECES, nx, zb, lanes), bf),
            pltpu.VMEM((oy, PIECES, nx, zb, lanes), bf),
            pltpu.VMEM((PIECES, nx, zb, lanes), f32),
            pltpu.VMEM((ox, PIECES, zb, lanes), bf),
            pltpu.VMEM((ox, PIECES, zb, lanes), bf),
            pltpu.VMEM((PIECES, nz // pair, CL_OWN, lanes), f32),
            pltpu.VMEM((PIECES, nz // pair, CL_OWN, lanes), f32),
            pltpu.VMEM((oz, PIECES, CL_OWN, lanes), bf),
            pltpu.VMEM((oz, PIECES, CL_OWN, lanes), bf),
            pltpu.VMEM((oz, PIECES, CL_OWN, lanes), bf),
            pltpu.VMEM((oz, PIECES, CL_OWN, lanes), bf),
            *dma(nx, CHUNKS),
            *dma(ox, CHUNKS),
            *dma(nx),
            *dma(ny),
            *dma(ox, PIECES),
            *dma(oy, PIECES),
            *dma(oy, PIECES),
            *dma(ox, PIECES),
            *dma(oz, PIECES),
            *dma(oz, PIECES),
            *dma(CHUNKS),
            pltpu.SemaphoreType.DMA,
            pltpu.SemaphoreType.DMA,
        ],
        compiler_params=pltpu.CompilerParams(
            collective_id=0, has_side_effects=True, vmem_limit_bytes=60 * 1024 * 1024
        ),
        name="pifa_step",
    )(tile_rows, tile_labels, cluster_ids.reshape(1, labels), features, tile_values)


def solution(mesh):
    return jax.shard_map(
        shards,
        mesh=mesh,
        in_specs=(
            P("inst", None),
            P(("inst", "lab")),
            P(("inst", "lab")),
            P(("inst", "lab"), None, None),
            P(("lab", "inst")),
        ),
        out_specs=(P(("lab", "inst"), None), P(("inst", "lab"), None)),
        check_vma=False,
    )
```

time: 39.1 us -> 37.7 us (0.964)
  local copies, waits for them, and re-layouts: 2.74 us -> 1.52 us
    unnamed x4 -> x2, local copies, waits for them, and re-layouts: 2.74 us -> 1.52 us
where the time goes in v2:
time: 37.7 us; the launch traced here: 37.6 us
  Pallas kernels  35.4 us (94%)
  local copies, waits for them, and re-layouts  1.52 us (4%)
  between operations  0.64 us (2%)
    pallas_call x1, Pallas kernels, shards(): pl.pallas_call(functools.partial(kernel, nx, ny, nz, pair), out_shape=(pl...  35.4 us
    unnamed x2, local copies, waits for them, and re-layouts  1.52 us

profile of v2, /device:TPU:0, one launch (start us, length us, event | category | flops | bytes accessed | tf_op | source)
XLA Modules:
  0.0 37.6 jit_solution(7128889120254946166)
XLA Ops:
  0.6 35.4 %pifa_step.1 = (f32[256,768]{1,0:T(8,128)S(1)}, f32[32,768]{1,0:T(8,128)S(1)}) custom-call(s32[4]{0:T(128)} %rows_ref.1, s32[4]{0:T(128)} %labs_ref.1, s32[1,256]{1,0:T(1,128)} %bitcast.1, bf16[512,768]{1,0:T(8,128)(2,1)} %feat_ref.1, bf16[4,256,256]{2,1,0:T(8,128)(2,1)} %val_ref.1), custom_call_target="tpu_custom_call" | custom-call | tf_op jit(solution)/shard_map/pifa_step/pallas_call | solution.py:343
  36.1 0.9 %copy.9 = f32[256,768]{1,0:T(8,128)} copy(f32[256,768]{1,0:T(8,128)S(1)} %get-tuple-element.2) | data formatting | bytes 1572864
  37.0 0.6 %copy.10 = f32[32,768]{1,0:T(8,128)} copy(f32[32,768]{1,0:T(8,128)S(1)} %get-tuple-element.3) | data formatting | bytes 196608

commit v3 on v2

--- a/solution.py
+++ b/solution.py
@@ -9,7 +9,8 @@
 
 CL_OWN = 32
 CHUNKS = 8
-PIECES = 3
+LAG = 3
+PIECES = 1
 MESH = pl.DeviceIdType.MESH
 
 
@@ -22,10 +23,10 @@
     rows_ref, labs_ref, ids_ref, feat_ref, val_ref,
     emb_ref, cen_ref,
     xn, vt, csend, crecv, xsend, xrecv, total, ebf, ids_far, picks,
-    ca_s, ca_r, xa_s, xa_r, acc_a, ya_s, ya_r,
-    cb_s, cb_r, yb_s, yb_r, acc_b, xb_s, xb_r,
+    xa_s, xa_r, acc_a, ya_s, ya_r,
+    yb_s, yb_r, acc_b, xb_s, xb_r,
     fin_a, fin_b, za_s, za_r, zb_s, zb_r,
-    s_core, r_core, s_x, r_x, s_ca, r_ca, s_cb, r_cb,
+    s_core, r_core, s_x, r_x,
     s_xa, r_xa, s_yb, r_yb, s_ya, r_ya, s_xb, r_xb, s_za, r_za, s_zb, r_zb, s_g, r_g, s_ids, r_ids,
 ):
     inst = lax.axis_index("inst")
@@ -87,13 +88,19 @@
         lhs = jnp.concatenate(pieces, axis=1)
         return jnp.dot(lhs, xn[...], preferred_element_type=jnp.float32)
 
-    ids_copy = remote(ids_ref, ids_far, s_ids, r_ids, pair_peer)
+    def ids_send(source, slot, peer):
+        return remote(source, ids_far.at[slot - 1], s_ids.at[slot - 1], r_ids.at[slot - 1], peer)
+
+    ids_sends = {pair: ids_send(ids_ref, pair, core_peer)}
+    if pair == 2:
+        ids_sends[1] = ids_send(ids_ref, 1, pair_peer)
+        ids_sends[3] = ids_send(ids_far.at[0], 3, core_peer)
 
     def meet():
         pl.semaphore_wait(barrier, len(peers))
-        if pair == 2:
-            ids_copy.start()
-            sent.append(ids_copy)
+        for slot, copy in ids_sends.items():
+            if slot <= pair:
+                copy.start()
 
     def core_send(d):
         xp = x_at(d)
@@ -146,19 +153,37 @@
         + lax.broadcasted_iota(jnp.int32, (zq_all, CL_OWN, tile), 1)
     )
 
-    def mark(ids, columns):
-        for which, cp in enumerate((other, c)):
-            for xp in range(nx):
-                for yp in range(ny):
-                    base = (((xp * 2 + cp) * nz + zr) * ny + yp) * CL_OWN
-                    hit = jnp.where(within + base == ids.reshape(1, 1, tile), 1.0, 0.0)
-                    picks[which, xp, yp, :, columns] = hit.reshape(zb, tile).astype(jnp.bfloat16)
-
-    gather = []
-    mark(ids_ref[...], pl.ds(0, tile))
-    if pair == 2:
-        ids_copy.wait_recv()
-        mark(ids_far[...], pl.ds(tile, tile))
+    def mark(ids, slot):
+        for xp in range(nx):
+            for yp in range(ny):
+                base = (((xp * 2 + c) * nz + zr) * ny + yp) * CL_OWN
+                hit = jnp.where(within + base == ids.reshape(1, 1, tile), 1.0, 0.0)
+                picks[xp, yp, :, slot * tile : (slot + 1) * tile] = hit.reshape(
+                    zb, tile
+                ).astype(jnp.bfloat16)
+
+    mark(ids_ref[...], 0)
+    for slot in range(1, 2 * pair):
+        ids_sends[slot].wait_recv()
+        if slot == 1 and pair == 2:
+            ids_sends[3].start()
+        mark(ids_far[slot - 1], slot)
+    sent += ids_sends.values()
+
+    def row_send(q, source, slot, peer):
+        copy = remote(
+            ebf.at[pl.ds(source * tile + q * part, part)],
+            ebf.at[pl.ds(slot * tile + q * part, part)],
+            s_g.at[slot - 1, q], r_g.at[slot - 1, q], peer,
+        )
+        copy.start()
+        gather[slot, q] = copy
+
+    gather = {}
+
+    def relay(q):
+        gather[1, q].wait_recv()
+        row_send(q, 1, 3, core_peer)
 
     for q in range(CHUNKS):
         rows = pl.ds(q * part, part)
@@ -170,50 +195,35 @@
         emb_ref[rows] = value
         ebf[rows] = value.astype(jnp.bfloat16)
         if pair == 2:
-            gather.append(
-                remote(
-                    ebf.at[rows], ebf.at[pl.ds(tile + q * part, part)],
-                    s_g.at[q], r_g.at[q], pair_peer,
-                )
-            )
-            gather[-1].start()
-    sent += gather
-
-    def sums_a(xp, which):
-        member = picks[which, xp].reshape(ny * zb, pair * tile)
+            row_send(q, 0, 1, pair_peer)
+            if q >= LAG:
+                relay(q - LAG)
+        row_send(q, 0, pair, core_peer)
+    if pair == 2:
+        for q in range(max(CHUNKS - LAG, 0), CHUNKS):
+            relay(q)
+    sent += gather.values()
+
+    def sums_a(xp):
+        member = picks[xp].reshape(ny * zb, 2 * pair * tile)
         out = jnp.dot(member, ebf[:, :half], preferred_element_type=jnp.float32)
         return out.reshape(ny, zb, half)
 
-    def sums_b(yp, which):
-        member = jnp.concatenate([picks[which, xp, yp] for xp in range(nx)], axis=0)
+    def sums_b(yp):
+        member = jnp.concatenate([picks[xp, yp] for xp in range(nx)], axis=0)
         out = jnp.dot(member, ebf[:, half:], preferred_element_type=jnp.float32)
         return out.reshape(nx, zb, half)
 
-    for copy in gather:
-        copy.wait_recv()
+    for (slot, _), copy in gather.items():
+        if slot > 1 or pair == 1:
+            copy.wait_recv()
 
     order = [*range(1, max(nx, ny)), 0]
-    core_a, core_b = {}, {}
-    for d in order:
-        if d < nx:
-            xp = x_at(d)
-            ca_s[xp] = sums_a(xp, 0).astype(jnp.bfloat16)
-            core_a[d] = remote(ca_s.at[xp], ca_r.at[xp], s_ca.at[xp], r_ca.at[xp], core_peer)
-            core_a[d].start()
-        if d < ny:
-            yp = y_at(d)
-            cb_s[yp] = sums_b(yp, 0).astype(jnp.bfloat16)
-            core_b[d] = remote(cb_s.at[yp], cb_r.at[yp], s_cb.at[yp], r_cb.at[yp], core_peer)
-            core_b[d].start()
-    sent += [*core_a.values(), *core_b.values()]
-
     xa, yb = {}, {}
     for d in order:
         if d < nx:
             xp = x_at(d)
-            mine = sums_a(xp, 1)
-            core_a[d].wait_recv()
-            mine = mine + ca_r[xp].astype(jnp.float32)
+            mine = sums_a(xp)
             for p in range(PIECES):
                 piece = mine[:, :, p * lanes : (p + 1) * lanes]
                 if d:
@@ -227,9 +237,7 @@
                     acc_a[p] = piece
         if d < ny:
             yp = y_at(d)
-            mine = sums_b(yp, 1)
-            core_b[d].wait_recv()
-            mine = mine + cb_r[yp].astype(jnp.float32)
+            mine = sums_b(yp)
             for p in range(PIECES):
                 piece = mine[:, :, p * lanes : (p + 1) * lanes]
                 if d:
@@ -356,18 +364,14 @@
             pltpu.VMEM((ox, tile, width), bf),
             pltpu.VMEM((ox, tile, width), bf),
             pltpu.VMEM((tile, width), f32),
-            pltpu.VMEM((pair * tile, width), bf),
-            pltpu.VMEM((1, tile), jnp.int32),
-            pltpu.VMEM((2, nx, ny, zb, pair * tile), bf),
-            pltpu.VMEM((nx, ny, zb, half), bf),
-            pltpu.VMEM((nx, ny, zb, half), bf),
+            pltpu.VMEM((2 * pair * tile, width), bf),
+            pltpu.VMEM((2 * pair - 1, 1, tile), jnp.int32),
+            pltpu.VMEM((nx, ny, zb, 2 * pair * tile), bf),
             pltpu.VMEM((ox, PIECES, ny, zb, lanes), bf),
             pltpu.VMEM((ox, PIECES, ny, zb, lanes), bf),
             pltpu.VMEM((PIECES, ny, zb, lanes), f32),
             pltpu.VMEM((oy, PIECES, zb, lanes), bf),
             pltpu.VMEM((oy, PIECES, zb, lanes), bf),
-            pltpu.VMEM((ny, nx, zb, half), bf),
-            pltpu.VMEM((ny, nx, zb, half), bf),
             pltpu.VMEM((oy, PIECES, nx, zb, lanes), bf),
             pltpu.VMEM((oy, PIECES, nx, zb, lanes), bf),
             pltpu.VMEM((PIECES, nx, zb, lanes), f32),
@@ -381,17 +385,14 @@
             pltpu.VMEM((oz, PIECES, CL_OWN, lanes), bf),
             *dma(nx, CHUNKS),
             *dma(ox, CHUNKS),
-            *dma(nx),
-            *dma(ny),
             *dma(ox, PIECES),
             *dma(oy, PIECES),
             *dma(oy, PIECES),
             *dma(ox, PIECES),
             *dma(oz, PIECES),
             *dma(oz, PIECES),
-            *dma(CHUNKS),
-            pltpu.SemaphoreType.DMA,
-            pltpu.SemaphoreType.DMA,
+            *dma(2 * pair - 1, CHUNKS),
+            *dma(2 * pair - 1),
         ],
         compiler_params=pltpu.CompilerParams(
             collective_id=0, has_side_effects=True, vmem_limit_bytes=60 * 1024 * 1024

time: 37.7 us -> 37.4 us (level)
  no operation moved by 1% of the time
where the time goes in v3:
time: 37.4 us; the launch traced here: 37.3 us
  Pallas kernels  35.1 us (94%)
  local copies, waits for them, and re-layouts  1.52 us (4%)
  between operations  0.64 us (2%)
    pallas_call x1, Pallas kernels, shards(): pl.pallas_call(functools.partial(kernel, nx, ny, nz, pair), out_shape=(pl...  35.1 us
    unnamed x2, local copies, waits for them, and re-layouts  1.52 us

profile of v3, /device:TPU:0, one launch (start us, length us, event | category | flops | bytes accessed | tf_op | source)
XLA Modules:
  0.0 37.3 jit_solution(13095428118727927001)
XLA Ops:
  0.6 35.1 %pifa_step.1 = (f32[256,768]{1,0:T(8,128)S(1)}, f32[32,768]{1,0:T(8,128)S(1)}) custom-call(s32[4]{0:T(128)} %rows_ref.1, s32[4]{0:T(128)} %labs_ref.1, s32[1,256]{1,0:T(1,128)} %bitcast.1, bf16[512,768]{1,0:T(8,128)(2,1)} %feat_ref.1, bf16[4,256,256]{2,1,0:T(8,128)(2,1)} %val_ref.1), custom_call_target="tpu_custom_call" | custom-call | tf_op jit(solution)/shard_map/pifa_step/pallas_call | solution.py:351
  35.8 0.9 %copy.9 = f32[256,768]{1,0:T(8,128)} copy(f32[256,768]{1,0:T(8,128)S(1)} %get-tuple-element.2) | data formatting | bytes 1572864
  36.6 0.6 %copy.10 = f32[32,768]{1,0:T(8,128)} copy(f32[32,768]{1,0:T(8,128)S(1)} %get-tuple-element.3) | data formatting | bytes 196608

commit v4 on v3

--- a/solution.py
+++ b/solution.py
@@ -22,7 +22,7 @@
     nx, ny, nz, pair,
     rows_ref, labs_ref, ids_ref, feat_ref, val_ref,
     emb_ref, cen_ref,
-    xn, vt, csend, crecv, xsend, xrecv, total, ebf, ids_far, picks,
+    xn, vt, csend, crecv, xsend, xrecv, total, ebf, ids_far, picks, pre_a, pre_b,
     xa_s, xa_r, acc_a, ya_s, ya_r,
     yb_s, yb_r, acc_b, xb_s, xb_r,
     fin_a, fin_b, za_s, za_r, zb_s, zb_r,
@@ -181,6 +181,18 @@
 
     gather = {}
 
+    def sums_a(xp, low, high):
+        keys = slice(low * tile, high * tile)
+        member = picks[xp, :, :, keys].reshape(ny * zb, (high - low) * tile)
+        out = jnp.dot(member, ebf[keys, :half], preferred_element_type=jnp.float32)
+        return out.reshape(ny, zb, half)
+
+    def sums_b(yp, low, high):
+        keys = slice(low * tile, high * tile)
+        member = jnp.concatenate([picks[xp, yp, :, keys] for xp in range(nx)], axis=0)
+        out = jnp.dot(member, ebf[keys, half:], preferred_element_type=jnp.float32)
+        return out.reshape(nx, zb, half)
+
     def relay(q):
         gather[1, q].wait_recv()
         row_send(q, 1, 3, core_peer)
@@ -199,23 +211,24 @@
             if q >= LAG:
                 relay(q - LAG)
         row_send(q, 0, pair, core_peer)
+    for xp in range(nx):
+        pre_a[xp] = sums_a(xp, 0, 1)
+    for yp in range(ny):
+        pre_b[yp] = sums_b(yp, 0, 1)
     if pair == 2:
         for q in range(max(CHUNKS - LAG, 0), CHUNKS):
             relay(q)
+        for q in range(CHUNKS):
+            gather[2, q].wait_recv()
+        for xp in range(nx):
+            pre_a[xp] += sums_a(xp, 1, 3)
+        for yp in range(ny):
+            pre_b[yp] += sums_b(yp, 1, 3)
     sent += gather.values()
 
-    def sums_a(xp):
-        member = picks[xp].reshape(ny * zb, 2 * pair * tile)
-        out = jnp.dot(member, ebf[:, :half], preferred_element_type=jnp.float32)
-        return out.reshape(ny, zb, half)
-
-    def sums_b(yp):
-        member = jnp.concatenate([picks[xp, yp] for xp in range(nx)], axis=0)
-        out = jnp.dot(member, ebf[:, half:], preferred_element_type=jnp.float32)
-        return out.reshape(nx, zb, half)
-
+    last = 2 * pair - 1
     for (slot, _), copy in gather.items():
-        if slot > 1 or pair == 1:
+        if slot == last:
             copy.wait_recv()
 
     order = [*range(1, max(nx, ny)), 0]
@@ -223,7 +236,7 @@
     for d in order:
         if d < nx:
             xp = x_at(d)
-            mine = sums_a(xp)
+            mine = pre_a[xp] + sums_a(xp, last, last + 1)
             for p in range(PIECES):
                 piece = mine[:, :, p * lanes : (p + 1) * lanes]
                 if d:
@@ -237,7 +250,7 @@
                     acc_a[p] = piece
         if d < ny:
             yp = y_at(d)
-            mine = sums_b(yp)
+            mine = pre_b[yp] + sums_b(yp, last, last + 1)
             for p in range(PIECES):
                 piece = mine[:, :, p * lanes : (p + 1) * lanes]
                 if d:
@@ -367,6 +380,8 @@
             pltpu.VMEM((2 * pair * tile, width), bf),
             pltpu.VMEM((2 * pair - 1, 1, tile), jnp.int32),
             pltpu.VMEM((nx, ny, zb, 2 * pair * tile), bf),
+            pltpu.VMEM((nx, ny, zb, half), f32),
+            pltpu.VMEM((ny, nx, zb, half), f32),
             pltpu.VMEM((ox, PIECES, ny, zb, lanes), bf),
             pltpu.VMEM((ox, PIECES, ny, zb, lanes), bf),
             pltpu.VMEM((PIECES, ny, zb, lanes), f32),

time: 37.4 us -> 37.3 us (level)
  no operation moved by 1% of the time
where the time goes in v4:
time: 37.3 us; the launch traced here: 37.1 us
  Pallas kernels  35 us (94%)
  local copies, waits for them, and re-layouts  1.52 us (4%)
  between operations  0.64 us (2%)
    pallas_call x1, Pallas kernels, shards(): pl.pallas_call(functools.partial(kernel, nx, ny, nz, pair), out_shape=(pl...  35 us
    unnamed x2, local copies, waits for them, and re-layouts  1.52 us

profile of v4, /device:TPU:0, one launch (start us, length us, event | category | flops | bytes accessed | tf_op | source)
XLA Modules:
  0.0 37.1 jit_solution(3047071897751494559)
XLA Ops:
  0.6 35.0 %pifa_step.1 = (f32[256,768]{1,0:T(8,128)S(1)}, f32[32,768]{1,0:T(8,128)S(1)}) custom-call(s32[4]{0:T(128)} %rows_ref.1, s32[4]{0:T(128)} %labs_ref.1, s32[1,256]{1,0:T(1,128)} %bitcast.1, bf16[512,768]{1,0:T(8,128)(2,1)} %feat_ref.1, bf16[4,256,256]{2,1,0:T(8,128)(2,1)} %val_ref.1), custom_call_target="tpu_custom_call" | custom-call | tf_op jit(solution)/shard_map/pifa_step/pallas_call | solution.py:364
  35.6 0.9 %copy.9 = f32[256,768]{1,0:T(8,128)} copy(f32[256,768]{1,0:T(8,128)S(1)} %get-tuple-element.2) | data formatting | bytes 1572864
  36.5 0.6 %copy.10 = f32[32,768]{1,0:T(8,128)} copy(f32[32,768]{1,0:T(8,128)S(1)} %get-tuple-element.3) | data formatting | bytes 196608

commit v5 on v2

--- a/solution.py
+++ b/solution.py
@@ -9,7 +9,7 @@
 
 CL_OWN = 32
 CHUNKS = 8
-PIECES = 3
+PIECES = 1
 MESH = pl.DeviceIdType.MESH
 
 

time: 37.7 us -> 37.1 us (0.984)
  Pallas kernels: 35.4 us -> 34.8 us
    pallas_call x1, Pallas kernels: 35.4 us -> 34.8 us  [shards(): pl.pallas_call(functools.partial(kernel, nx, ny, nz, pair), out_shape=(pl...]
where the time goes in v5:
time: 37.1 us; the launch traced here: 37 us
  Pallas kernels  34.8 us (94%)
  local copies, waits for them, and re-layouts  1.52 us (4%)
  between operations  0.64 us (2%)
    pallas_call x1, Pallas kernels, shards(): pl.pallas_call(functools.partial(kernel, nx, ny, nz, pair), out_shape=(pl...  34.8 us
    unnamed x2, local copies, waits for them, and re-layouts  1.52 us

profile of v5, /device:TPU:0, one launch (start us, length us, event | category | flops | bytes accessed | tf_op | source)
XLA Modules:
  0.0 37.0 jit_solution(10534544044759545815)
XLA Ops:
  0.6 34.8 %pifa_step.1 = (f32[256,768]{1,0:T(8,128)S(1)}, f32[32,768]{1,0:T(8,128)S(1)}) custom-call(s32[4]{0:T(128)} %rows_ref.1, s32[4]{0:T(128)} %labs_ref.1, s32[1,256]{1,0:T(1,128)} %bitcast.1, bf16[512,768]{1,0:T(8,128)(2,1)} %feat_ref.1, bf16[4,256,256]{2,1,0:T(8,128)(2,1)} %val_ref.1), custom_call_target="tpu_custom_call" | custom-call | tf_op jit(solution)/shard_map/pifa_step/pallas_call | solution.py:343
  35.4 0.9 %copy.9 = f32[256,768]{1,0:T(8,128)} copy(f32[256,768]{1,0:T(8,128)S(1)} %get-tuple-element.2) | data formatting | bytes 1572864
  36.3 0.6 %copy.10 = f32[32,768]{1,0:T(8,128)} copy(f32[32,768]{1,0:T(8,128)S(1)} %get-tuple-element.3) | data formatting | bytes 196608
